TPU v7x, 32 devices: a whole 2x2x4 slice. The times are simulated.
32 devices in a mesh: domain: 2 (over x), fsdp: 16 (over z, y, core).
Axes of the slice: x: 2, y: 2, z: 4, core: 2. Of those that a mesh axis runs over, the one named last changes fastest.
Arguments:
- gradients: bfloat16 [2, 4, 4096, 512], P('domain', None, 'fsdp')
- row_counts: int32 [4], replicated, may hold values from 2048 to 4096, as said below
- domain_ids: int32 [2], replicated, may hold values from 0 to 7
- domain_weights: float32 [8], replicated, may hold values from 0.2 to 2
Outputs:
- updates: float32 [4, 4096, 512], P('domain', 'fsdp')
- new_weights: float32 [8], replicated
Inputs may be any that keep to these rules, and one draw needn't show every extreme that they name: `row_counts`: each matrix has 4096 or 2048 rows, and both counts occur.
All inputs are finite; a program needn't handle non-finite values.
Results may differ from a plain program's by a relative error of at most 0.0071.
Values may be sent and summed in bfloat16 or wider, within the bound.
No kernel may reach another device: no remote copies, remote signals or barrier semaphores. Data moves between devices by JAX's collectives and lax.ppermute only.
A program may use at most 64 MiB of HBM per device.

v0:
```python
import math
import jax
import jax.numpy as jnp
from jax import lax
from jax.sharding import PartitionSpec as P

NS_ITERS = 3
OWNERS = 8
COEF_A = 3.4445
COEF_B = -4.775
COEF_C = 2.0315
MUON_SCALE = 0.2
ETA = 4.0


def partner(shard, axis, stride):
    return lax.ppermute(shard, axis, [(i, i ^ 1 << stride) for i in range(lax.axis_size(axis))])


def group_mixing(domain_ids, domain_weights, kind_count):
    weight_share = domain_weights / jnp.sum(domain_weights)
    onehot = (domain_ids[:, None] == jnp.arange(kind_count, dtype=jnp.int32)[None, :]).astype(
        jnp.float32
    )
    counts = jnp.sum(onehot, axis=0)
    per_member = weight_share / jnp.maximum(counts, 1.0)
    group_mix = jnp.sum(onehot * per_member[None, :], axis=1)
    return (weight_share, onehot, counts, group_mix)


def summed_gram(iterate):
    gram_total = lax.dot_general(
        iterate, iterate, (((0,), (0,)), ((), ())), preferred_element_type=jnp.float32
    )
    for bit_pos in range(OWNERS.bit_length() - 1):
        gram_total = gram_total + partner(gram_total, "fsdp", bit_pos)
    return gram_total


def newton_steps(iterate):
    for repeat in range(NS_ITERS):
        gram_full = lax.optimization_barrier(summed_gram(iterate).astype(jnp.bfloat16))
        square = jnp.dot(gram_full, gram_full, preferred_element_type=jnp.float32)
        poly_term = (COEF_B * gram_full.astype(jnp.float32) + COEF_C * square).astype(jnp.bfloat16)
        iterate = lax.optimization_barrier(
            (
                COEF_A * iterate.astype(jnp.float32)
                + jnp.dot(iterate, poly_term, preferred_element_type=jnp.float32)
            ).astype(jnp.bfloat16)
        )
    return iterate


def share_scores(aligned, squares, norm_slots):
    return lax.psum((aligned, squares, norm_slots), ("domain", "fsdp"))


def body(gradients, row_counts, domain_ids, domain_weights):
    groups = lax.axis_size("domain")
    shards = lax.axis_size("fsdp")
    matrices = row_counts.shape[0]
    rows_src = gradients.shape[2]
    columns = gradients.shape[3]
    per_domain = matrices // groups
    sub_rows = rows_src // OWNERS
    own_rows = shards * sub_rows
    full_rows = rows_src * shards
    domain_pos = lax.axis_index("domain")
    shard_pos = lax.axis_index("fsdp")
    weight_share, onehot, counts, group_mix = group_mixing(
        domain_ids, domain_weights, domain_weights.shape[0]
    )
    blocks = lax.all_to_all(
        gradients.reshape(1, groups, per_domain, rows_src, columns),
        "domain",
        split_axis=1,
        concat_axis=0,
        tiled=True,
    )
    blocks = blocks.reshape(groups, per_domain, rows_src, columns)
    global_rows = shard_pos * rows_src + jnp.arange(rows_src, dtype=jnp.int32)
    limits = lax.dynamic_slice_in_dim(row_counts, domain_pos * per_domain, per_domain, 0)
    row_mask = (global_rows[None, :] < limits[:, None])[None, :, :, None]
    masked = jnp.where(row_mask, blocks.astype(jnp.float32), jnp.zeros((), jnp.float32))
    combined = jnp.sum(group_mix[:, None, None, None] * masked, axis=0)
    aligned = jnp.sum(masked * combined[None], axis=(1, 2, 3))
    squares = jnp.sum(masked * masked, axis=(1, 2, 3))
    block_squares = jnp.sum(combined * combined, axis=(1, 2))
    norm_slots = lax.dynamic_update_slice_in_dim(
        jnp.zeros((matrices,), jnp.float32), block_squares, domain_pos * per_domain, 0
    )
    aligned, squares, norm_slots = share_scores(aligned, squares, norm_slots)
    frob_norm = (
        jnp.sqrt(lax.dynamic_slice_in_dim(norm_slots, domain_pos * per_domain, per_domain, 0))
        + 1e-07
    )
    scaled = (combined / frob_norm[:, None, None]).astype(jnp.bfloat16)
    scaled = scaled.reshape(shards, 1, sub_rows, columns)
    start_rows = lax.all_to_all(scaled, "fsdp", split_axis=0, concat_axis=1, tiled=True)
    start_rows = lax.optimization_barrier(start_rows.reshape(own_rows, columns))
    finished = newton_steps(start_rows)
    returned = lax.all_to_all(
        finished.reshape(1, shards, sub_rows, columns),
        "fsdp",
        split_axis=1,
        concat_axis=0,
        tiled=True,
    )
    returned = returned.reshape(per_domain, rows_src, columns)
    updates = returned.astype(jnp.float32) * (MUON_SCALE * math.sqrt(full_rows))
    total_sq = jnp.sum(norm_slots)
    cosine = aligned / (jnp.sqrt(squares) * jnp.sqrt(total_sq) + 1e-06)
    score = jnp.sum(onehot * cosine[:, None], axis=0) / jnp.maximum(counts, 1.0)
    raised = weight_share * jnp.exp(ETA * score)
    return (updates, raised / jnp.sum(raised))


def solution(mesh):
    placed = (P("domain", None, "fsdp", None), P(), P(), P())
    return jax.shard_map(
        body,
        mesh=mesh,
        in_specs=placed,
        out_specs=(P("domain", "fsdp", None), P()),
        check_vma=False,
    )
```

profile of v0, /device:TPU:0, one launch (start us, length us, event | category | flops | bytes accessed | tf_op | source)
XLA Modules:
  0.0 265.7 jit_solution(6877497156156330844)
XLA Ops:
  0.7 4.4 %all-to-all-start = ((bf16[1,2,2,256,512]{4,3,2,0,1:T(8,128)(2,1)}), bf16[1,2,2,256,512]{4,3,2,0,1:T(8,128)(2,1)S(1)}, u32[]{:S(2)}, u32[]{:S(2)}) async-start(bf16[1,2,2,256,512]{4,3,2,0,1:T(8,128)(2,1)} %bitcast.31), calls=%async_computation | async-start | bytes 2097152 | tf_op jit(solution)/shard_map/all_to_all | solution.py:73
  5.1 0.6 reduce_sum.92
  5.8 0.7 multiply_divide_fusion
  6.7 12.7 %all-to-all-done = bf16[1,2,2,256,512]{4,3,2,0,1:T(8,128)(2,1)S(1)} async-done(((bf16[1,2,2,256,512]{4,3,2,0,1:T(8,128)(2,1)}), bf16[1,2,2,256,512]{4,3,2,0,1:T(8,128)(2,1)S(1)}, u32[]{:S(2)}, u32[]{:S(2)}) %all-to-all-start) | async-done | bytes 1048608 | tf_op jit(solution)/shard_map/all_to_all | solution.py:73
  19.5 0.3 fusion.3
  19.8 0.2 multiply_reduce_fusion
  20.0 0.2 dynamic_update_slice.3
  20.2 0.7 fusion.5
  20.9 39.8 %all-reduce = (f32[4]{0:T(128)S(1)}, f32[2]{0:T(128)S(1)}, f32[2]{0:T(128)S(1)}) all-reduce(f32[4]{0:T(128)S(1)} %dynamic_update_slice.3, f32[2]{0:T(128)S(1)} %get-tuple-element.3, f32[2]{0:T(128)S(1)} %get-tuple-element.2), channel_id=1, replica_groups=mesh['domain'=2,'fsdp'=16] {'domain','fsdp'}, use_global_device_ids=true, to_apply=%region_5.6 | all-reduce | flops 8 | bytes 64 | tf_op jit(solution)/shard_map/psum | solution.py:55
  60.7 0.6 reduce_sum.100
  62.2 0.2 divide_convert_fusion
  62.4 19.5 %all_to_all.12 = bf16[16,1,32,512]{3,2,1,0:T(8,128)(2,1)S(1)} all-to-all(bf16[16,1,32,512]{3,2,1,0:T(8,128)(2,1)S(1)} %divide_convert_fusion), channel_id=1, replica_groups=mesh['domain'=2,'fsdp'=16] {'fsdp'}, dimensions={0} | all-to-all | bytes 1048576 | tf_op jit(solution)/shard_map/all_to_all | solution.py:99
  81.9 0.5 fusion.22
  82.4 0.2 collective-permute-start
  82.6 2.5 collective-permute-done
  85.1 0.2 add.76
  85.3 1.1 collective-permute-start.1
  86.4 24.2 %collective-permute-done.1 = f32[512,512]{1,0:T(8,128)S(1)} collective-permute-done((f32[512,512]{1,0:T(8,128)S(1)}, f32[512,512]{1,0:T(8,128)S(1)}, u32[]{:S(2)}, u32[]{:S(2)}) %collective-permute-start.1) | collective-permute-done | bytes 1048608 | tf_op jit(solution)/shard_map/ppermute | solution.py:17
  110.6 0.2 add.77
  110.8 1.8 collective-permute-start.2
  112.6 22.8 %collective-permute-done.2 = f32[512,512]{1,0:T(8,128)S(1)} collective-permute-done((f32[512,512]{1,0:T(8,128)S(1)}, f32[512,512]{1,0:T(8,128)S(1)}, u32[]{:S(2)}, u32[]{:S(2)}) %collective-permute-start.2) | collective-permute-done | bytes 1048608 | tf_op jit(solution)/shard_map/ppermute | solution.py:17
  135.4 0.3 add_convert_fusion.5
  135.7 0.8 fusion.6
  136.5 0.5 fusion.23
  137.0 2.6 collective-permute-done.3
  139.7 0.2 add.81
  139.9 1.3 collective-permute-start.4
  141.2 23.9 %collective-permute-done.4 = f32[512,512]{1,0:T(8,128)S(1)} collective-permute-done((f32[512,512]{1,0:T(8,128)S(1)}, f32[512,512]{1,0:T(8,128)S(1)}, u32[]{:S(2)}, u32[]{:S(2)}) %collective-permute-start.4) | collective-permute-done | bytes 1048608 | tf_op jit(solution)/shard_map/ppermute | solution.py:17
  165.2 0.2 add.82
  165.4 1.8 collective-permute-start.5
  167.2 22.6 %collective-permute-done.5 = f32[512,512]{1,0:T(8,128)S(1)} collective-permute-done((f32[512,512]{1,0:T(8,128)S(1)}, f32[512,512]{1,0:T(8,128)S(1)}, u32[]{:S(2)}, u32[]{:S(2)}) %collective-permute-start.5) | collective-permute-done | bytes 1048608 | tf_op jit(solution)/shard_map/ppermute | solution.py:17
  189.8 0.3 add_convert_fusion.3
  190.0 0.8 fusion.7
  190.8 0.5 fusion.24
  191.4 2.6 collective-permute-done.6
  194.0 0.2 add.86
  194.2 1.3 collective-permute-start.7
  195.6 23.9 %collective-permute-done.7 = f32[512,512]{1,0:T(8,128)S(1)} collective-permute-done((f32[512,512]{1,0:T(8,128)S(1)}, f32[512,512]{1,0:T(8,128)S(1)}, u32[]{:S(2)}, u32[]{:S(2)}) %collective-permute-start.7) | collective-permute-done | bytes 1048608 | tf_op jit(solution)/shard_map/ppermute | solution.py:17
  219.5 0.2 add.87
  219.7 1.8 collective-permute-start.8
  221.5 22.6 %collective-permute-done.8 = f32[512,512]{1,0:T(8,128)S(1)} collective-permute-done((f32[512,512]{1,0:T(8,128)S(1)}, f32[512,512]{1,0:T(8,128)S(1)}, u32[]{:S(2)}, u32[]{:S(2)}) %collective-permute-start.8) | collective-permute-done | bytes 1048608 | tf_op jit(solution)/shard_map/ppermute | solution.py:17
  244.1 0.3 add_convert_fusion.1
  244.4 1.6 fusion.8
  245.9 4.4 %all-to-all-start.2 = ((bf16[1,16,32,512]{3,2,0,1:T(8,128)(2,1)}), bf16[1,16,32,512]{3,2,0,1:T(8,128)(2,1)S(1)}, u32[]{:S(2)}, u32[]{:S(2)}) async-start(bf16[1,16,32,512]{3,2,0,1:T(8,128)(2,1)} %bitcast.5), calls=%async_computation.2 | async-start | bytes 1048576 | tf_op jit(solution)/shard_map/all_to_all | solution.py:102
  250.4 1.3 fusion.21
  251.8 1.2 broadcast_divide_fusion
  253.0 11.6 %all-to-all-done.2 = bf16[1,16,32,512]{3,2,0,1:T(8,128)(2,1)S(1)} async-done(((bf16[1,16,32,512]{3,2,0,1:T(8,128)(2,1)}), bf16[1,16,32,512]{3,2,0,1:T(8,128)(2,1)S(1)}, u32[]{:S(2)}, u32[]{:S(2)}) %all-to-all-start.2) | async-done | bytes 524320 | tf_op jit(solution)/shard_map/all_to_all | solution.py:102
  264.6 1.1 convert_multiply_fusion
  (18 shorter events, 0.9 us)
Async XLA Ops:
  0.6 4.4 %copy-start.2 = (s32[2]{0:T(128)S(1)}, s32[2]{0:T(128)}, u32[]{:S(2)}) copy-start(s32[2]{0:T(128)} %param.6) | copy-start | bytes 28
  0.6 4.5 %copy-start = (f32[8]{0:T(128)S(1)}, f32[8]{0:T(128)}, u32[]{:S(2)}) copy-start(f32[8]{0:T(128)} %param.7) | copy-start | bytes 100
  0.7 5.1 %copy-start.1 = (s32[4]{0:T(128)S(1)}, s32[4]{0:T(128)}, u32[]{:S(2)}) copy-start(s32[4]{0:T(128)} %param.5) | copy-start | bytes 52
  0.7 18.8 %all-to-all-start = ((bf16[1,2,2,256,512]{4,3,2,0,1:T(8,128)(2,1)}), bf16[1,2,2,256,512]{4,3,2,0,1:T(8,128)(2,1)S(1)}, u32[]{:S(2)}, u32[]{:S(2)}) async-start(bf16[1,2,2,256,512]{4,3,2,0,1:T(8,128)(2,1)} %bitcast.31), calls=%async_computation | async-start | bytes 2097152 | tf_op jit(solution)/shard_map/all_to_all | solution.py:73
  82.4 2.7 %collective-permute-start = (f32[512,512]{1,0:T(8,128)S(1)}, f32[512,512]{1,0:T(8,128)S(1)}, u32[]{:S(2)}, u32[]{:S(2)}) collective-permute-start(f32[512,512]{1,0:T(8,128)S(1)} %fusion.22), channel_id=1, source_target_pairs={{0,1},{1,0},{2,3},{3,2},{4,5},{5,4},{6,7},{7,6},{8,9},{9,8},{10,11... | collective-permute-start | bytes 3145736 | tf_op jit(solution)/shard_map/ppermute | solution.py:17
  85.3 25.3 %collective-permute-start.1 = (f32[512,512]{1,0:T(8,128)S(1)}, f32[512,512]{1,0:T(8,128)S(1)}, u32[]{:S(2)}, u32[]{:S(2)}) collective-permute-start(f32[512,512]{1,0:T(8,128)S(1)} %add.76), channel_id=1, source_target_pairs={{0,2},{1,3},{2,0},{3,1},{4,6},{5,7},{6,4},{7,5},{8,10},{9,11},{10,... | collective-permute-start | bytes 3145736 | tf_op jit(solution)/shard_map/ppermute | solution.py:17
  110.8 24.7 %collective-permute-start.2 = (f32[512,512]{1,0:T(8,128)S(1)}, f32[512,512]{1,0:T(8,128)S(1)}, u32[]{:S(2)}, u32[]{:S(2)}) collective-permute-start(f32[512,512]{1,0:T(8,128)S(1)} %add.77), channel_id=1, source_target_pairs={{0,4},{1,5},{2,6},{3,7},{4,0},{5,1},{6,2},{7,3},{8,12},{9,13},{10,... | collective-permute-start | bytes 3145736 | tf_op jit(solution)/shard_map/ppermute | solution.py:17
  137.0 2.7 %collective-permute-start.3 = (f32[512,512]{1,0:T(8,128)S(1)}, f32[512,512]{1,0:T(8,128)S(1)}, u32[]{:S(2)}, u32[]{:S(2)}) collective-permute-start(f32[512,512]{1,0:T(8,128)S(1)} %fusion.23), channel_id=1, source_target_pairs={{0,1},{1,0},{2,3},{3,2},{4,5},{5,4},{6,7},{7,6},{8,9},{9,8},{10,11... | collective-permute-start | bytes 3145736 | tf_op jit(solution)/shard_map/ppermute | solution.py:17
  139.9 25.3 %collective-permute-start.4 = (f32[512,512]{1,0:T(8,128)S(1)}, f32[512,512]{1,0:T(8,128)S(1)}, u32[]{:S(2)}, u32[]{:S(2)}) collective-permute-start(f32[512,512]{1,0:T(8,128)S(1)} %add.81), channel_id=1, source_target_pairs={{0,2},{1,3},{2,0},{3,1},{4,6},{5,7},{6,4},{7,5},{8,10},{9,11},{10,... | collective-permute-start | bytes 3145736 | tf_op jit(solution)/shard_map/ppermute | solution.py:17
  165.4 24.4 %collective-permute-start.5 = (f32[512,512]{1,0:T(8,128)S(1)}, f32[512,512]{1,0:T(8,128)S(1)}, u32[]{:S(2)}, u32[]{:S(2)}) collective-permute-start(f32[512,512]{1,0:T(8,128)S(1)} %add.82), channel_id=1, source_target_pairs={{0,4},{1,5},{2,6},{3,7},{4,0},{5,1},{6,2},{7,3},{8,12},{9,13},{10,... | collective-permute-start | bytes 3145736 | tf_op jit(solution)/shard_map/ppermute | solution.py:17
  191.3 2.7 %collective-permute-start.6 = (f32[512,512]{1,0:T(8,128)S(1)}, f32[512,512]{1,0:T(8,128)S(1)}, u32[]{:S(2)}, u32[]{:S(2)}) collective-permute-start(f32[512,512]{1,0:T(8,128)S(1)} %fusion.24), channel_id=1, source_target_pairs={{0,1},{1,0},{2,3},{3,2},{4,5},{5,4},{6,7},{7,6},{8,9},{9,8},{10,11... | collective-permute-start | bytes 3145736 | tf_op jit(solution)/shard_map/ppermute | solution.py:17
  194.2 25.3 %collective-permute-start.7 = (f32[512,512]{1,0:T(8,128)S(1)}, f32[512,512]{1,0:T(8,128)S(1)}, u32[]{:S(2)}, u32[]{:S(2)}) collective-permute-start(f32[512,512]{1,0:T(8,128)S(1)} %add.86), channel_id=1, source_target_pairs={{0,2},{1,3},{2,0},{3,1},{4,6},{5,7},{6,4},{7,5},{8,10},{9,11},{10,... | collective-permute-start | bytes 3145736 | tf_op jit(solution)/shard_map/ppermute | solution.py:17
  219.7 24.4 %collective-permute-start.8 = (f32[512,512]{1,0:T(8,128)S(1)}, f32[512,512]{1,0:T(8,128)S(1)}, u32[]{:S(2)}, u32[]{:S(2)}) collective-permute-start(f32[512,512]{1,0:T(8,128)S(1)} %add.87), channel_id=1, source_target_pairs={{0,4},{1,5},{2,6},{3,7},{4,0},{5,1},{6,2},{7,3},{8,12},{9,13},{10,... | collective-permute-start | bytes 3145736 | tf_op jit(solution)/shard_map/ppermute | solution.py:17
  245.9 18.7 %all-to-all-start.2 = ((bf16[1,16,32,512]{3,2,0,1:T(8,128)(2,1)}), bf16[1,16,32,512]{3,2,0,1:T(8,128)(2,1)S(1)}, u32[]{:S(2)}, u32[]{:S(2)}) async-start(bf16[1,16,32,512]{3,2,0,1:T(8,128)(2,1)} %bitcast.5), calls=%async_computation.2 | async-start | bytes 1048576 | tf_op jit(solution)/shard_map/all_to_all | solution.py:102
where the time goes:
time: 266 us
  waiting for transfers between devices  172 us (65%)
  blocking collectives  59.3 us (22%)
  starting transfers between devices  18.3 us (7%)
  other arithmetic  9.43 us (4%)
  matrix products  4.55 us (2%)
    ppermute x9, waiting for transfers between devices, partner(): lax.ppermute(shard, axis, [(i, i ^ 1 << stride) for i in range(lax.axis_s...  148 us
    psum x1, blocking collectives, share_scores(): return lax.psum((aligned, squares, norm_slots), ('domain', 'fsdp'))  39.8 us
    all_to_all x1, blocking collectives, body(): lax.all_to_all(scaled, 'fsdp', split_axis=0, concat_axis=1, tiled=True)  19.5 us
    all_to_all x1, waiting for transfers between devices, body(): lax.all_to_all(gradients.reshape(1, groups, per_domain, rows_src, columns...  12.7 us
    all_to_all x1, waiting for transfers between devices, body(): lax.all_to_all(finished.reshape(1, shards, sub_rows, columns), 'fsdp', sp...  11.6 us
    ppermute x9, starting transfers between devices, partner(): lax.ppermute(shard, axis, [(i, i ^ 1 << stride) for i in range(lax.axis_s...  9.5 us
  transfers between devices with their start and end apart: 11, of which 11 were waited for; matrix products, arithmetic and copies ran while one was open for 2% of the time, Pallas kernels for 0%

commit v1 on v0

--- a/solution.py
+++ b/solution.py
@@ -52,7 +52,7 @@
 
 
 def share_scores(aligned, squares, norm_slots):
-    return lax.psum((aligned, squares, norm_slots), ("domain", "fsdp"))
+    return lax.psum(lax.psum((aligned, squares, norm_slots), "fsdp"), "domain")
 
 
 def body(gradients, row_counts, domain_ids, domain_weights):

time: 266 us -> 262 us (0.985)
  blocking collectives: 59.3 us -> 54.7 us
    psum x1 -> x2, blocking collectives: 39.8 us -> 37.8 us  [share_scores(): return lax.psum(lax.psum((aligned, squares, norm_slots), 'fsdp'), 'domain')]
where the time goes in v1:
time: 262 us; the launch traced here: 261 us
  waiting for transfers between devices  172 us (66%)
  blocking collectives  54.7 us (21%)
  starting transfers between devices  18.1 us (7%)
  other arithmetic  9.43 us (4%)
  matrix products  4.54 us (2%)
    ppermute x9, waiting for transfers between devices, partner(): lax.ppermute(shard, axis, [(i, i ^ 1 << stride) for i in range(lax.axis_s...  148 us
    psum x2, blocking collectives, share_scores(): return lax.psum(lax.psum((aligned, squares, norm_slots), 'fsdp'), 'domain')  37.8 us
    all_to_all x1, blocking collectives, body(): lax.all_to_all(scaled, 'fsdp', split_axis=0, concat_axis=1, tiled=True)  16.9 us
    all_to_all x1, waiting for transfers between devices, body(): lax.all_to_all(gradients.reshape(1, groups, per_domain, rows_src, columns...  12.7 us
    all_to_all x1, waiting for transfers between devices, body(): lax.all_to_all(finished.reshape(1, shards, sub_rows, columns), 'fsdp', sp...  11.6 us
    ppermute x9, starting transfers between devices, partner(): lax.ppermute(shard, axis, [(i, i ^ 1 << stride) for i in range(lax.axis_s...  9.42 us
  transfers between devices with their start and end apart: 11, of which 11 were waited for; matrix products, arithmetic and copies ran while one was open for 2% of the time, Pallas kernels for 0%

profile of v1, /device:TPU:0, one launch (start us, length us, event | category | flops | bytes accessed | tf_op | source)
XLA Modules:
  0.0 261.1 jit_solution(4482531152342902894)
XLA Ops:
  0.7 4.4 %all-to-all-start = ((bf16[1,2,2,256,512]{4,3,2,0,1:T(8,128)(2,1)}), bf16[1,2,2,256,512]{4,3,2,0,1:T(8,128)(2,1)S(1)}, u32[]{:S(2)}, u32[]{:S(2)}) async-start(bf16[1,2,2,256,512]{4,3,2,0,1:T(8,128)(2,1)} %bitcast.31), calls=%async_computation | async-start | bytes 2097152 | tf_op jit(solution)/shard_map/all_to_all | solution.py:73
  5.1 0.6 reduce_sum.92
  5.8 0.7 multiply_divide_fusion
  6.7 12.7 %all-to-all-done = bf16[1,2,2,256,512]{4,3,2,0,1:T(8,128)(2,1)S(1)} async-done(((bf16[1,2,2,256,512]{4,3,2,0,1:T(8,128)(2,1)}), bf16[1,2,2,256,512]{4,3,2,0,1:T(8,128)(2,1)S(1)}, u32[]{:S(2)}, u32[]{:S(2)}) %all-to-all-start) | async-done | bytes 1048608 | tf_op jit(solution)/shard_map/all_to_all | solution.py:73
  19.5 0.3 fusion.3
  19.8 0.2 multiply_reduce_fusion
  20.0 0.2 dynamic_update_slice.3
  20.2 0.7 fusion.5
  20.9 32.9 %all-reduce = (f32[4]{0:T(128)S(1)}, f32[2]{0:T(128)S(1)}, f32[2]{0:T(128)S(1)}) all-reduce(f32[4]{0:T(128)S(1)} %dynamic_update_slice.3, f32[2]{0:T(128)S(1)} %get-tuple-element.3, f32[2]{0:T(128)S(1)} %get-tuple-element.2), channel_id=1, replica_groups=mesh['domain'=2,'fsdp'=16] {'fsdp'}, use_global_device_ids=true, to_apply=%region_5.6 | all-reduce | flops 8 | bytes 64 | tf_op jit(solution)/shard_map/psum | solution.py:55
  53.8 4.9 %all-reduce.1 = (f32[4]{0:T(128)S(1)}, f32[2]{0:T(128)S(1)}, f32[2]{0:T(128)S(1)}) all-reduce(f32[4]{0:T(128)S(1)} %get-tuple-element.4, f32[2]{0:T(128)S(1)} %get-tuple-element.5, f32[2]{0:T(128)S(1)} %get-tuple-element.6), channel_id=1, replica_groups=mesh['domain'=2,'fsdp'=16] {'domain'}, use_global_device_ids=true, to_apply=%region_6.7 | all-reduce | flops 8 | bytes 64 | tf_op jit(solution)/shard_map/psum | solution.py:55
  58.7 0.6 reduce_sum.100
  60.2 0.2 divide_convert_fusion
  60.4 16.9 %all_to_all.12 = bf16[16,1,32,512]{3,2,1,0:T(8,128)(2,1)S(1)} all-to-all(bf16[16,1,32,512]{3,2,1,0:T(8,128)(2,1)S(1)} %divide_convert_fusion), channel_id=1, replica_groups=mesh['domain'=2,'fsdp'=16] {'fsdp'}, dimensions={0} | all-to-all | bytes 1048576 | tf_op jit(solution)/shard_map/all_to_all | solution.py:99
  77.3 0.5 fusion.22
  78.0 2.5 collective-permute-done
  80.5 0.2 add.82
  80.7 1.1 collective-permute-start.1
  81.8 24.2 %collective-permute-done.1 = f32[512,512]{1,0:T(8,128)S(1)} collective-permute-done((f32[512,512]{1,0:T(8,128)S(1)}, f32[512,512]{1,0:T(8,128)S(1)}, u32[]{:S(2)}, u32[]{:S(2)}) %collective-permute-start.1) | collective-permute-done | bytes 1048608 | tf_op jit(solution)/shard_map/ppermute | solution.py:17
  106.0 0.2 add.83
  106.2 1.8 collective-permute-start.2
  108.0 22.8 %collective-permute-done.2 = f32[512,512]{1,0:T(8,128)S(1)} collective-permute-done((f32[512,512]{1,0:T(8,128)S(1)}, f32[512,512]{1,0:T(8,128)S(1)}, u32[]{:S(2)}, u32[]{:S(2)}) %collective-permute-start.2) | collective-permute-done | bytes 1048608 | tf_op jit(solution)/shard_map/ppermute | solution.py:17
  130.8 0.3 add_convert_fusion.5
  131.1 0.8 fusion.6
  131.9 0.5 fusion.23
  132.4 2.6 %collective-permute-done.3 = f32[512,512]{1,0:T(8,128)S(1)} collective-permute-done((f32[512,512]{1,0:T(8,128)S(1)}, f32[512,512]{1,0:T(8,128)S(1)}, u32[]{:S(2)}, u32[]{:S(2)}) %collective-permute-start.3) | collective-permute-done | bytes 1048608 | tf_op jit(solution)/shard_map/ppermute | solution.py:17
  135.1 0.2 add.87
  135.3 1.3 collective-permute-start.4
  136.6 23.9 %collective-permute-done.4 = f32[512,512]{1,0:T(8,128)S(1)} collective-permute-done((f32[512,512]{1,0:T(8,128)S(1)}, f32[512,512]{1,0:T(8,128)S(1)}, u32[]{:S(2)}, u32[]{:S(2)}) %collective-permute-start.4) | collective-permute-done | bytes 1048608 | tf_op jit(solution)/shard_map/ppermute | solution.py:17
  160.5 0.2 add.88
  160.8 1.8 collective-permute-start.5
  162.6 22.6 %collective-permute-done.5 = f32[512,512]{1,0:T(8,128)S(1)} collective-permute-done((f32[512,512]{1,0:T(8,128)S(1)}, f32[512,512]{1,0:T(8,128)S(1)}, u32[]{:S(2)}, u32[]{:S(2)}) %collective-permute-start.5) | collective-permute-done | bytes 1048608 | tf_op jit(solution)/shard_map/ppermute | solution.py:17
  185.2 0.3 add_convert_fusion.3
  185.4 0.8 fusion.7
  186.2 0.5 fusion.24
  186.8 2.6 %collective-permute-done.6 = f32[512,512]{1,0:T(8,128)S(1)} collective-permute-done((f32[512,512]{1,0:T(8,128)S(1)}, f32[512,512]{1,0:T(8,128)S(1)}, u32[]{:S(2)}, u32[]{:S(2)}) %collective-permute-start.6) | collective-permute-done | bytes 1048608 | tf_op jit(solution)/shard_map/ppermute | solution.py:17
  189.4 0.2 add.92
  189.6 1.3 collective-permute-start.7
  190.9 24.0 %collective-permute-done.7 = f32[512,512]{1,0:T(8,128)S(1)} collective-permute-done((f32[512,512]{1,0:T(8,128)S(1)}, f32[512,512]{1,0:T(8,128)S(1)}, u32[]{:S(2)}, u32[]{:S(2)}) %collective-permute-start.7) | collective-permute-done | bytes 1048608 | tf_op jit(solution)/shard_map/ppermute | solution.py:17
  214.9 0.2 add.93
  215.1 1.8 collective-permute-start.8
  216.9 22.6 %collective-permute-done.8 = f32[512,512]{1,0:T(8,128)S(1)} collective-permute-done((f32[512,512]{1,0:T(8,128)S(1)}, f32[512,512]{1,0:T(8,128)S(1)}, u32[]{:S(2)}, u32[]{:S(2)}) %collective-permute-start.8) | collective-permute-done | bytes 1048608 | tf_op jit(solution)/shard_map/ppermute | solution.py:17
  239.5 0.3 add_convert_fusion.1
  239.8 1.6 fusion.8
  241.3 4.3 %all-to-all-start.2 = ((bf16[1,16,32,512]{3,2,0,1:T(8,128)(2,1)}), bf16[1,16,32,512]{3,2,0,1:T(8,128)(2,1)S(1)}, u32[]{:S(2)}, u32[]{:S(2)}) async-start(bf16[1,16,32,512]{3,2,0,1:T(8,128)(2,1)} %bitcast.5), calls=%async_computation.2 | async-start | bytes 1048576 | tf_op jit(solution)/shard_map/all_to_all | solution.py:102
  245.8 1.3 fusion.21
  247.1 1.2 broadcast_divide_fusion
  248.3 11.6 %all-to-all-done.2 = bf16[1,16,32,512]{3,2,0,1:T(8,128)(2,1)S(1)} async-done(((bf16[1,16,32,512]{3,2,0,1:T(8,128)(2,1)}), bf16[1,16,32,512]{3,2,0,1:T(8,128)(2,1)S(1)}, u32[]{:S(2)}, u32[]{:S(2)}) %all-to-all-start.2) | async-done | bytes 524320 | tf_op jit(solution)/shard_map/all_to_all | solution.py:102
  260.0 1.1 convert_multiply_fusion
  (19 shorter events, 1.1 us)
Async XLA Ops:
  0.6 4.4 %copy-start.2 = (s32[2]{0:T(128)S(1)}, s32[2]{0:T(128)}, u32[]{:S(2)}) copy-start(s32[2]{0:T(128)} %param.6) | copy-start | bytes 28
  0.6 4.5 %copy-start = (f32[8]{0:T(128)S(1)}, f32[8]{0:T(128)}, u32[]{:S(2)}) copy-start(f32[8]{0:T(128)} %param.7) | copy-start | bytes 100
  0.7 5.1 %copy-start.1 = (s32[4]{0:T(128)S(1)}, s32[4]{0:T(128)}, u32[]{:S(2)}) copy-start(s32[4]{0:T(128)} %param.5) | copy-start | bytes 52
  0.7 18.8 %all-to-all-start = ((bf16[1,2,2,256,512]{4,3,2,0,1:T(8,128)(2,1)}), bf16[1,2,2,256,512]{4,3,2,0,1:T(8,128)(2,1)S(1)}, u32[]{:S(2)}, u32[]{:S(2)}) async-start(bf16[1,2,2,256,512]{4,3,2,0,1:T(8,128)(2,1)} %bitcast.31), calls=%async_computation | async-start | bytes 2097152 | tf_op jit(solution)/shard_map/all_to_all | solution.py:73
  77.8 2.7 %collective-permute-start = (f32[512,512]{1,0:T(8,128)S(1)}, f32[512,512]{1,0:T(8,128)S(1)}, u32[]{:S(2)}, u32[]{:S(2)}) collective-permute-start(f32[512,512]{1,0:T(8,128)S(1)} %fusion.22), channel_id=1, source_target_pairs={{0,1},{1,0},{2,3},{3,2},{4,5},{5,4},{6,7},{7,6},{8,9},{9,8},{10,11... | collective-permute-start | bytes 3145736 | tf_op jit(solution)/shard_map/ppermute | solution.py:17
  80.7 25.3 %collective-permute-start.1 = (f32[512,512]{1,0:T(8,128)S(1)}, f32[512,512]{1,0:T(8,128)S(1)}, u32[]{:S(2)}, u32[]{:S(2)}) collective-permute-start(f32[512,512]{1,0:T(8,128)S(1)} %add.82), channel_id=1, source_target_pairs={{0,2},{1,3},{2,0},{3,1},{4,6},{5,7},{6,4},{7,5},{8,10},{9,11},{10,... | collective-permute-start | bytes 3145736 | tf_op jit(solution)/shard_map/ppermute | solution.py:17
  106.2 24.6 %collective-permute-start.2 = (f32[512,512]{1,0:T(8,128)S(1)}, f32[512,512]{1,0:T(8,128)S(1)}, u32[]{:S(2)}, u32[]{:S(2)}) collective-permute-start(f32[512,512]{1,0:T(8,128)S(1)} %add.83), channel_id=1, source_target_pairs={{0,4},{1,5},{2,6},{3,7},{4,0},{5,1},{6,2},{7,3},{8,12},{9,13},{10,... | collective-permute-start | bytes 3145736 | tf_op jit(solution)/shard_map/ppermute | solution.py:17
  132.3 2.7 %collective-permute-start.3 = (f32[512,512]{1,0:T(8,128)S(1)}, f32[512,512]{1,0:T(8,128)S(1)}, u32[]{:S(2)}, u32[]{:S(2)}) collective-permute-start(f32[512,512]{1,0:T(8,128)S(1)} %fusion.23), channel_id=1, source_target_pairs={{0,1},{1,0},{2,3},{3,2},{4,5},{5,4},{6,7},{7,6},{8,9},{9,8},{10,11... | collective-permute-start | bytes 3145736 | tf_op jit(solution)/shard_map/ppermute | solution.py:17
  135.3 25.3 %collective-permute-start.4 = (f32[512,512]{1,0:T(8,128)S(1)}, f32[512,512]{1,0:T(8,128)S(1)}, u32[]{:S(2)}, u32[]{:S(2)}) collective-permute-start(f32[512,512]{1,0:T(8,128)S(1)} %add.87), channel_id=1, source_target_pairs={{0,2},{1,3},{2,0},{3,1},{4,6},{5,7},{6,4},{7,5},{8,10},{9,11},{10,... | collective-permute-start | bytes 3145736 | tf_op jit(solution)/shard_map/ppermute | solution.py:17
  160.8 24.4 %collective-permute-start.5 = (f32[512,512]{1,0:T(8,128)S(1)}, f32[512,512]{1,0:T(8,128)S(1)}, u32[]{:S(2)}, u32[]{:S(2)}) collective-permute-start(f32[512,512]{1,0:T(8,128)S(1)} %add.88), channel_id=1, source_target_pairs={{0,4},{1,5},{2,6},{3,7},{4,0},{5,1},{6,2},{7,3},{8,12},{9,13},{10,... | collective-permute-start | bytes 3145736 | tf_op jit(solution)/shard_map/ppermute | solution.py:17
  186.7 2.7 %collective-permute-start.6 = (f32[512,512]{1,0:T(8,128)S(1)}, f32[512,512]{1,0:T(8,128)S(1)}, u32[]{:S(2)}, u32[]{:S(2)}) collective-permute-start(f32[512,512]{1,0:T(8,128)S(1)} %fusion.24), channel_id=1, source_target_pairs={{0,1},{1,0},{2,3},{3,2},{4,5},{5,4},{6,7},{7,6},{8,9},{9,8},{10,11... | collective-permute-start | bytes 3145736 | tf_op jit(solution)/shard_map/ppermute | solution.py:17
  189.6 25.3 %collective-permute-start.7 = (f32[512,512]{1,0:T(8,128)S(1)}, f32[512,512]{1,0:T(8,128)S(1)}, u32[]{:S(2)}, u32[]{:S(2)}) collective-permute-start(f32[512,512]{1,0:T(8,128)S(1)} %add.92), channel_id=1, source_target_pairs={{0,2},{1,3},{2,0},{3,1},{4,6},{5,7},{6,4},{7,5},{8,10},{9,11},{10,... | collective-permute-start | bytes 3145736 | tf_op jit(solution)/shard_map/ppermute | solution.py:17
  215.1 24.4 %collective-permute-start.8 = (f32[512,512]{1,0:T(8,128)S(1)}, f32[512,512]{1,0:T(8,128)S(1)}, u32[]{:S(2)}, u32[]{:S(2)}) collective-permute-start(f32[512,512]{1,0:T(8,128)S(1)} %add.93), channel_id=1, source_target_pairs={{0,4},{1,5},{2,6},{3,7},{4,0},{5,1},{6,2},{7,3},{8,12},{9,13},{10,... | collective-permute-start | bytes 3145736 | tf_op jit(solution)/shard_map/ppermute | solution.py:17
  241.3 18.6 %all-to-all-start.2 = ((bf16[1,16,32,512]{3,2,0,1:T(8,128)(2,1)}), bf16[1,16,32,512]{3,2,0,1:T(8,128)(2,1)S(1)}, u32[]{:S(2)}, u32[]{:S(2)}) async-start(bf16[1,16,32,512]{3,2,0,1:T(8,128)(2,1)} %bitcast.5), calls=%async_computation.2 | async-start | bytes 1048576 | tf_op jit(solution)/shard_map/all_to_all | solution.py:102
